TPU v7x, 512 devices: a whole 4x8x8 slice. The times are simulated.
512 devices in a mesh: seq: 64 (over z, x, core), head: 8 (over y).
Axes of the slice: x: 4, y: 8, z: 8, core: 2. Of those that a mesh axis runs over, the one named last changes fastest.
Arguments:
- query_states: bfloat16 [16384, 4096], P(('seq', 'head')), may hold values from -8 to 8
- key_states: bfloat16 [16384, 4096], P(('seq', 'head')), may hold values from -8 to 8
- value_states: bfloat16 [16384, 4096], P(('seq', 'head')), may hold values from -8 to 8
- out_grad: bfloat16 [16384, 4096], P(('seq', 'head')), may hold values from -6 to 6
Outputs:
- attended: bfloat16 [16384, 4096], P('seq', 'head')
- query_grad: bfloat16 [16384, 4096], P('seq', 'head')
- key_grad: bfloat16 [16384, 4096], P('seq', 'head')
- value_grad: bfloat16 [16384, 4096], P('seq', 'head')
All inputs are finite; a program needn't handle non-finite values.
Results may differ from a plain program's by a relative error of at most 0.025.
Values may be sent and summed in bfloat16 or wider, within the bound.
A program may use at most 64 MiB of HBM per device.

v0:
```python
import jax
import jax.numpy as jnp
import numpy as np
from jax import lax
from jax.sharding import Mesh
from jax.sharding import PartitionSpec as P

HEAD_DIM = 128
BLOCK = 128


def seq_parts(mesh):
    column = mesh.devices[:, 0]
    count = column.shape[0]
    try:
        cores = len({d.core_on_chip for d in column})
        xs = len({d.coords[0] for d in column})
    except AttributeError:
        return (("s0", count),)
    parts = [("sz", count // (xs * cores)), ("sx", xs), ("sc", cores)]
    if parts[0][1] * xs * cores != count:
        return (("s0", count),)
    return tuple((p for p in parts if p[1] > 1)) or (("s0", count),)


def make_local(parts):
    seq = tuple((name for name, _ in parts))
    seq_count = int(np.prod([size for _, size in parts]))

    def hpsum(value):
        for name in reversed(seq):
            value = lax.psum(value, name)
        return value

    def hgather(value):
        for name in reversed(seq):
            value = lax.all_gather(value, name, axis=0, tiled=True)
        return value

    def shifted(value, steps):
        leading, last = (max(0, -steps), min(seq_count, seq_count - steps))
        return lax.ppermute(value, seq, [(s, s + steps) for s in range(leading, last)])

    def local(query_states, key_states, value_states, out_grad):
        stacked = jnp.stack([query_states, key_states, value_states, out_grad])
        stacked = lax.all_to_all(stacked, "head", split_axis=2, concat_axis=1, tiled=True)
        local_rows = stacked.shape[1]
        head_count = stacked.shape[2] // HEAD_DIM
        block_count = local_rows // BLOCK
        position = lax.axis_index(seq)
        total_blocks = block_count * seq_count
        inverse_square_root = HEAD_DIM ** (-0.5)
        query_states, key_states, value_states, out_grad = (
            stacked[0],
            stacked[1],
            stacked[2],
            stacked[3],
        )

        def as_blocks(array):
            return array.reshape(block_count, BLOCK, head_count, HEAD_DIM)

        def as_heads(array):
            return array.reshape(array.shape[0], head_count, HEAD_DIM)

        leading = stacked[:, :BLOCK]
        leading = jnp.where(position == 0, leading, jnp.zeros_like(leading))
        leading = hpsum(leading)
        glob_query = as_heads(leading[0])
        glob_key = as_heads(leading[1])
        glob_value = as_heads(leading[2])
        glob_grad = as_heads(leading[3])
        kv = stacked[1:3]
        from_before = shifted(kv[:, local_rows - BLOCK :], 1)
        from_after = shifted(kv[:, :BLOCK], -1)
        extended = jnp.concatenate([from_before, kv, from_after], axis=1)

        def windows(rows_ext, shared):
            spread = jnp.broadcast_to(shared[None], (block_count, BLOCK, head_count, HEAD_DIM))
            return jnp.concatenate(
                [
                    spread,
                    as_blocks(rows_ext[:local_rows]),
                    as_blocks(rows_ext[BLOCK : BLOCK + local_rows]),
                    as_blocks(rows_ext[2 * BLOCK :]),
                ],
                1,
            )

        window_key_rows = windows(extended[0], glob_key)
        window_value_rows = windows(extended[1], glob_value)
        block_ids = position * block_count + jnp.arange(block_count)
        allowed = jnp.stack(
            [block_ids >= 2, block_ids >= 1, block_ids >= 0, block_ids + 1 < total_blocks], 1
        )
        allowed = jnp.repeat(allowed, BLOCK, axis=1)[:, None, None, :]
        live_rows = (block_ids != 0)[:, None, None, None]
        query_blocks = as_blocks(query_states)
        grad_blocks = as_blocks(out_grad)
        logit_scores = (
            jnp.einsum(
                "cqhd,ckhd->chqk", query_blocks, window_key_rows, preferred_element_type=jnp.float32
            )
            * inverse_square_root
        )
        logit_scores = jnp.where(allowed, logit_scores, -1e30)
        row_top = jnp.max(logit_scores, -1, keepdims=True)
        log_total = row_top + jnp.log(jnp.sum(jnp.exp(logit_scores - row_top), -1, keepdims=True))
        weights = jnp.where(allowed & live_rows, jnp.exp(logit_scores - log_total), 0.0)
        probabilities = weights.astype(jnp.bfloat16)
        window_output = jnp.einsum(
            "chqk,ckhd->cqhd", probabilities, window_value_rows, preferred_element_type=jnp.float32
        ).astype(jnp.bfloat16)
        local_keys = as_heads(key_states)
        local_values = as_heads(value_states)
        glob_scores = (
            jnp.einsum("qhd,khd->hqk", glob_query, local_keys, preferred_element_type=jnp.float32)
            * inverse_square_root
        )
        local_top = jnp.max(glob_scores, -1)
        local_exp = jnp.exp(glob_scores - local_top[:, :, None])
        local_sum = jnp.sum(local_exp, -1)
        local_out = jnp.einsum(
            "hqk,khd->hqd",
            local_exp,
            local_values.astype(jnp.float32),
            preferred_element_type=jnp.float32,
        )
        local_delta = jnp.sum(local_out * glob_grad.astype(jnp.float32).transpose(1, 0, 2), -1)
        stats = hgather(jnp.stack([local_top, local_sum, local_delta])[None])
        glob_top = jnp.max(stats[:, 0], 0)
        rescale = jnp.exp(stats[:, 0] - glob_top[None])
        glob_total = jnp.sum(rescale * stats[:, 1], 0)
        glob_log = glob_top + jnp.log(glob_total)
        glob_delta = jnp.sum(rescale * stats[:, 2], 0) / glob_total
        glob_weights = jnp.exp(glob_scores - glob_log[:, :, None])
        glob_probs = glob_weights.astype(jnp.bfloat16)
        glob_part = jnp.einsum(
            "hqk,khd->qhd", glob_probs, local_values, preferred_element_type=jnp.float32
        )
        glob_dprob = jnp.einsum(
            "qhd,khd->hqk", glob_grad, local_values, preferred_element_type=jnp.float32
        )
        glob_dscore = (glob_weights * (glob_dprob - glob_delta[:, :, None])).astype(jnp.bfloat16)
        glob_dquery_part = (
            jnp.einsum("hqk,khd->qhd", glob_dscore, local_keys, preferred_element_type=jnp.float32)
            * inverse_square_root
        )
        key_from_glob = (
            jnp.einsum("hqk,qhd->khd", glob_dscore, glob_query, preferred_element_type=jnp.float32)
            * inverse_square_root
        )
        value_from_glob = jnp.einsum(
            "hqk,qhd->khd", glob_probs, glob_grad, preferred_element_type=jnp.float32
        )
        band_delta = jnp.sum(
            grad_blocks.astype(jnp.float32) * window_output.astype(jnp.float32), -1
        ).transpose(0, 2, 1)
        probability_gradient = jnp.einsum(
            "cqhd,ckhd->chqk", grad_blocks, window_value_rows, preferred_element_type=jnp.float32
        )
        score_gradient = (weights * (probability_gradient - band_delta[:, :, :, None])).astype(
            jnp.bfloat16
        )
        window_query_gradient = (
            jnp.einsum(
                "chqk,ckhd->cqhd",
                score_gradient,
                window_key_rows,
                preferred_element_type=jnp.float32,
            )
            * inverse_square_root
        )
        window_key_gradient = (
            jnp.einsum(
                "chqk,cqhd->ckhd", score_gradient, query_blocks, preferred_element_type=jnp.float32
            )
            * inverse_square_root
        )
        window_value_gradient = jnp.einsum(
            "chqk,cqhd->ckhd", probabilities, grad_blocks, preferred_element_type=jnp.float32
        )
        stacked_grads = jnp.stack([window_key_gradient, window_value_gradient]).reshape(
            2, block_count, 4, BLOCK, head_count, HEAD_DIM
        )
        glob_piece = jnp.sum(stacked_grads[:, :, 0], 1)
        before = stacked_grads[:, :, 1]
        middle = stacked_grads[:, :, 2]
        after = stacked_grads[:, :, 3]
        empty_block = jnp.zeros((2, 1, BLOCK, head_count, HEAD_DIM), jnp.float32)
        inner = (
            middle
            + jnp.concatenate([before[:, 1:], empty_block], 1)
            + jnp.concatenate([empty_block, after[:, :-1]], 1)
        )
        from_right = shifted(before[:, 0].astype(jnp.bfloat16), -1).astype(jnp.float32)
        from_left = shifted(after[:, -1].astype(jnp.bfloat16), 1).astype(jnp.float32)
        inner = inner.at[:, 0].add(from_left)
        inner = inner.at[:, -1].add(from_right)
        glob_out, glob_dquery, glob_dkey, glob_dvalue = hpsum(
            (glob_part, glob_dquery_part, glob_piece[0], glob_piece[1])
        )
        glob_out = glob_out.astype(jnp.bfloat16)
        local_grads = inner.reshape(2, local_rows, head_count, HEAD_DIM) + jnp.stack(
            [key_from_glob, value_from_glob]
        )
        is_first = ((jnp.arange(local_rows) < BLOCK) & (position == 0))[:, None, None]

        def padded(array):
            return jnp.concatenate(
                [array, jnp.zeros((local_rows - BLOCK,) + array.shape[1:], array.dtype)], 0
            )

        key_grad = local_grads[0] + jnp.where(is_first, padded(glob_dkey), 0.0)
        value_grad = local_grads[1] + jnp.where(is_first, padded(glob_dvalue), 0.0)
        query_grad = jnp.where(
            is_first,
            padded(glob_dquery),
            window_query_gradient.reshape(local_rows, head_count, HEAD_DIM),
        )
        attended = jnp.where(
            is_first, padded(glob_out), window_output.reshape(local_rows, head_count, HEAD_DIM)
        )
        return (
            attended.reshape(local_rows, -1),
            query_grad.reshape(local_rows, -1).astype(jnp.bfloat16),
            key_grad.reshape(local_rows, -1).astype(jnp.bfloat16),
            value_grad.reshape(local_rows, -1).astype(jnp.bfloat16),
        )

    return (local, seq)


def solution(mesh):
    parts = seq_parts(mesh)
    heads = mesh.shape["head"]
    names = tuple((name for name, _ in parts))
    sizes = tuple((size for _, size in parts))
    split_mesh = Mesh(mesh.devices.reshape(sizes + (heads,)), names + ("head",))
    local, seq = make_local(parts)
    spec_in = P(seq + ("head",), None)
    spec_out = P(seq, "head")
    return jax.shard_map(
        local, mesh=split_mesh, in_specs=(spec_in,) * 4, out_specs=(spec_out,) * 4, check_vma=False
    )
```

profile of v0, /device:TPU:2, one launch (start us, length us, event | category | flops | bytes accessed | tf_op | source)
XLA Modules:
  0.0 490.2 jit_solution(11910787131558376043)
XLA Ops:
  8.5 4.6 copy.152
  13.1 7.8 %reshape.257 = bf16[8,2,32768]{2,1,0:T(2,128)(2,1)} reshape(bf16[4096,4,32]{2,1,0:T(4,128)(2,1)} %bitcast.155) | data formatting | bytes 2097152
  20.9 7.1 %all-to-all-start = ((bf16[8,2,32768]{2,1,0:T(2,128)(2,1)}), bf16[8,2,32768]{2,1,0:T(2,128)(2,1)S(1)}, u32[]{:S(2)}, u32[]{:S(2)}) async-start(bf16[8,2,32768]{2,1,0:T(2,128)(2,1)} %reshape.257), calls=%async_computation | async-start | bytes 2097152 | tf_op jit(solution)/shard_map/all_to_all | solution.py:46
  28.1 28.7 %all-to-all-done = bf16[8,2,32768]{2,1,0:T(2,128)(2,1)S(1)} async-done(((bf16[8,2,32768]{2,1,0:T(2,128)(2,1)}), bf16[8,2,32768]{2,1,0:T(2,128)(2,1)S(1)}, u32[]{:S(2)}, u32[]{:S(2)}) %all-to-all-start) | async-done | bytes 1048608 | tf_op jit(solution)/shard_map/all_to_all | solution.py:46
  56.8 4.5 reshape.258
  61.3 5.5 %copy.199 = bf16[4,32,8,512]{3,1,2,0:T(8,128)(2,1)S(1)} copy(bf16[4,32,8,512]{1,0,3,2:T(4,128)(2,1)} %bitcast.153) | data formatting | bytes 2097152 | tf_op jit(solution)/shard_map/all_to_all | solution.py:46
  67.7 34.6 %all-reduce.18.cloned.1.call-done = bf16[4,128,512]{2,1,0:T(8,128)(2,1)} async-done(((bf16[4,128,512]{2,1,0:T(8,128)(2,1)}), bf16[4,128,512]{2,1,0:T(8,128)(2,1)}) %all-reduce.18.cloned.1.call-update) | async-done | bytes 524304 | tf_op jit(solution)/shard_map/psum | solution.py:32
  102.5 4.7 copy.198
  107.5 2.2 collective-permute-start
  109.7 3.4 collective-permute-start.1
  113.1 46.0 %all-reduce.20.cloned.1.call-done = bf16[4,128,512]{2,1,0:T(8,128)(2,1)} async-done(((bf16[4,128,512]{2,1,0:T(8,128)(2,1)}), bf16[4,128,512]{2,1,0:T(8,128)(2,1)}) %all-reduce.20.cloned.1.call-update) | async-done | bytes 524304 | tf_op jit(solution)/shard_map/psum | solution.py:32
  164.3 78.4 %all-reduce.22.cloned.1.call-done = bf16[4,128,512]{2,1,0:T(8,128)(2,1)} async-done(((bf16[4,128,512]{2,1,0:T(8,128)(2,1)}), bf16[4,128,512]{2,1,0:T(8,128)(2,1)}) %all-reduce.22.cloned.1.call-update) | async-done | bytes 524304 | tf_op jit(solution)/shard_map/psum | solution.py:32
  245.8 1.8 all-gather
  247.7 11.9 %all_gather.10 = f32[8,3,4,128]{3,2,1,0:T(4,128)S(1)} all-gather(f32[2,3,4,128]{3,2,1,0:T(4,128)S(1)} %bitcast.176), channel_id=1, replica_groups=mesh['sz'=8,'sx'=4,'sc'=2,'head'=8] {'sx'}, dimensions={0}, use_global_device_ids=true | all-gather | bytes 61440 | tf_op jit(solution)/shard_map/all_gather | solution.py:37
  259.6 25.1 %all_gather.11 = f32[64,3,4,128]{3,2,1,0:T(4,128)S(1)} all-gather(f32[8,3,4,128]{3,2,1,0:T(4,128)S(1)} %all_gather.10), channel_id=1, replica_groups=mesh['sz'=8,'sx'=4,'sc'=2,'head'=8] {'sz'}, dimensions={0}, use_global_device_ids=true | all-gather | bytes 442368 | tf_op jit(solution)/shard_map/all_gather | solution.py:37
  297.7 2.0 copy_dynamic-update-slice_fusion.1
  304.7 1.9 collective-permute-start.2
  307.4 3.6 collective-permute-start.3
  311.1 25.9 %all-reduce.28.cloned.1.call-done = (f32[128,4,128]{0,2,1:T(8,128)}, f32[128,4,128]{0,2,1:T(8,128)}, f32[128,4,128]{0,2,1:T(8,128)}, f32[128,4,128]{0,2,1:T(8,128)}) async-done(((f32[128,4,128]{0,2,1:T(8,128)}, f32[128,4,128]{0,2,1:T(8,128)}, f32[128,4,128]{0,2,1:T(8,128)}, f32[128,4,128]{0,2,1:T(8,128)}), (f32[128,4,128]{0,2,1:T(8,128)}, f32[128,4,128]{0,2,1:T(8,128)}, f32[128,4,128]{0,2,1:T(8,128)}, ...) | async-done | bytes 1048592 | tf_op jit(solution)/shard_map/psum | solution.py:32
  337.2 2.6 fusion.1
  347.2 12.0 %scatter-add.9 = f32[2,2,128,4,128]{2,1,4,3,0:T(2,128)S(1)} dynamic-update-slice(f32[2,2,128,4,128]{2,1,4,3,0:T(2,128)S(1)} %copy.191, f32[2,1,128,4,128]{2,1,4,3,0:T(1,128)S(1)} %add.147, s32[]{:T(128)} %constant.93.clone.1, s32[]{:T(128)} %constant.98.clone.1, s32[]{:T(128)} %constant.93.clone.1, s32[]{:T(128)} %constant.93.clone.1, s32[]{:T(128)} %constant.93.clone.1) | dynamic-update-slice | bytes 1048580 | tf_op jit(solution)/shard_map/scatter-add | solution.py:199
  360.1 37.1 %all-reduce.26.cloned.1.call-done = (f32[128,4,128]{0,2,1:T(8,128)}, f32[128,4,128]{0,2,1:T(8,128)}, f32[128,4,128]{0,2,1:T(8,128)}, f32[128,4,128]{0,2,1:T(8,128)}) async-done(((f32[128,4,128]{0,2,1:T(8,128)}, f32[128,4,128]{0,2,1:T(8,128)}, f32[128,4,128]{0,2,1:T(8,128)}, f32[128,4,128]{0,2,1:T(8,128)}), (f32[128,4,128]{0,2,1:T(8,128)}, f32[128,4,128]{0,2,1:T(8,128)}, f32[128,4,128]{0,2,1:T(8,128)}, ...) | async-done | bytes 1048592 | tf_op jit(solution)/shard_map/psum | solution.py:32
  398.5 39.7 %all-reduce.29 = (bf16[128,4,128]{0,2,1:T(8,128)(2,1)S(1)}, bf16[128,4,128]{0,2,1:T(8,128)(2,1)S(1)}) all-reduce(f32[128,4,128]{0,2,1:T(8,128)S(1)} %copy-done.14, f32[128,4,128]{0,2,1:T(8,128)} %get-tuple-element.55), channel_id=1, replica_groups=mesh['sz'=8,'sx'=4,'sc'=2,'head'=8] {'sz'}, use_global_device_ids=true, to_apply=%region_10.11 | all-reduce | flops 131072 | bytes 786432 | tf_op jit(solution)/shard_map/psum | solution.py:32
  440.0 40.6 %all-reduce.24.cloned.1.call-done = (f32[128,4,128]{0,2,1:T(8,128)}, f32[128,4,128]{0,2,1:T(8,128)}) async-done(((f32[128,4,128]{0,2,1:T(8,128)}, f32[128,4,128]{0,2,1:T(8,128)}), (f32[128,4,128]{0,2,1:T(8,128)}, f32[128,4,128]{0,2,1:T(8,128)})) %all-reduce.24.cloned.1.call-update) | async-done | bytes 524304 | tf_op jit(solution)/shard_map/psum | solution.py:32
  (144 shorter events, 43.8 us)
Async XLA Ops:
  20.9 35.8 %all-to-all-start = ((bf16[8,2,32768]{2,1,0:T(2,128)(2,1)}), bf16[8,2,32768]{2,1,0:T(2,128)(2,1)S(1)}, u32[]{:S(2)}, u32[]{:S(2)}) async-start(bf16[8,2,32768]{2,1,0:T(2,128)(2,1)} %reshape.257), calls=%async_computation | async-start | bytes 2097152 | tf_op jit(solution)/shard_map/all_to_all | solution.py:46
  28.0 74.3 %all-reduce.18.cloned.1.call-start = ((), (), s32[]{:S(2)}) async-start(), calls=%async_computation.1 | async-start | bytes 1048576 | tf_op jit(solution)/shard_map/psum | solution.py:32
  67.6 91.4 %all-reduce.20.cloned.1.call-start = ((), (), s32[]{:S(2)}) async-start(), calls=%async_computation.2 | async-start | bytes 1048576 | tf_op jit(solution)/shard_map/psum | solution.py:32
  102.3 140.3 %all-reduce.22.cloned.1.call-start = ((), (), s32[]{:S(2)}) async-start(), calls=%async_computation.3 | async-start | bytes 1048576 | tf_op jit(solution)/shard_map/psum | solution.py:32
  107.5 53.7 %collective-permute-start = (bf16[2,128,512]{2,1,0:T(8,128)(2,1)S(1)}, bf16[2,128,512]{2,1,0:T(8,128)(2,1)}, u32[]{:S(2)}, u32[]{:S(2)}) collective-permute-start(bf16[2,128,512]{2,1,0:T(8,128)(2,1)S(1)} %get-tuple-element.83), channel_id=1, source_target_pairs={{0,8},{8,16},{16,24},{24,32},{32,40},{40,48},{48,56},{56,64},{64,7... | collective-permute-start | bytes 786440 | tf_op jit(solution)/shard_map/ppermute | solution.py:42
  109.7 51.5 %collective-permute-start.1 = (bf16[2,128,512]{2,1,0:T(8,128)(2,1)S(1)}, bf16[2,128,512]{2,1,0:T(8,128)(2,1)}, u32[]{:S(2)}, u32[]{:S(2)}) collective-permute-start(bf16[2,128,512]{2,1,0:T(8,128)(2,1)S(1)} %get-tuple-element.84), channel_id=1, source_target_pairs={{8,0},{16,8},{24,16},{32,24},{40,32},{48,40},{56,48},{64,56},{72,6... | collective-permute-start | bytes 786440 | tf_op jit(solution)/shard_map/ppermute | solution.py:42
  159.1 177.9 %all-reduce.28.cloned.1.call-start = ((), (), s32[]{:S(2)}) async-start(), calls=%async_computation.6 | async-start | bytes 2097152 | tf_op jit(solution)/shard_map/psum | solution.py:32
  160.7 126.5 %copy-start.9 = (bf16[2,128,4,128]{3,1,2,0:T(8,128)(2,1)}, bf16[2,128,4,128]{3,1,2,0:T(8,128)(2,1)S(1)}, u32[]{:S(2)}) copy-start(bf16[2,128,4,128]{3,1,2,0:T(8,128)(2,1)S(1)} %copy.175) | copy-start | bytes 786436
  162.5 124.7 %copy-start.10 = (bf16[2,128,4,128]{3,1,2,0:T(8,128)(2,1)}, bf16[2,128,4,128]{3,1,2,0:T(8,128)(2,1)S(1)}, u32[]{:S(2)}) copy-start(bf16[2,128,4,128]{3,1,2,0:T(8,128)(2,1)S(1)} %copy.174) | copy-start | bytes 786436
  164.3 122.9 %copy-start.11 = (bf16[2,128,4,128]{3,1,2,0:T(8,128)(2,1)}, bf16[2,128,4,128]{3,1,2,0:T(8,128)(2,1)S(1)}, u32[]{:S(2)}) copy-start(bf16[2,128,4,128]{3,1,2,0:T(8,128)(2,1)S(1)} %copy.176) | copy-start | bytes 786436
  244.8 41.1 %copy-start.3 = (bf16[1,128,512]{1,2,0:T(8,128)(2,1)}, bf16[1,128,512]{1,2,0:T(8,128)(2,1)S(1)}, u32[]{:S(2)}) copy-start(bf16[1,128,512]{1,2,0:T(8,128)(2,1)S(1)} %copy.156) | copy-start | bytes 393220
  297.7 2.2 copy-start.1
  300.2 2.0 copy-start
  303.0 94.3 %all-reduce.26.cloned.1.call-start = ((), (), s32[]{:S(2)}) async-start(), calls=%async_computation.5 | async-start | bytes 2097152 | tf_op jit(solution)/shard_map/psum | solution.py:32
  304.7 40.0 %collective-permute-start.2 = (bf16[2,128,4,128]{1,3,2,0:T(8,128)(2,1)}, bf16[2,128,4,128]{1,3,2,0:T(8,128)(2,1)S(1)}, u32[]{:S(2)}, u32[]{:S(2)}) collective-permute-start(bf16[2,128,4,128]{1,3,2,0:T(8,128)(2,1)} %fusion.17), channel_id=1, source_target_pairs={{0,8},{8,16},{16,24},{24,32},{32,40},{40,48},{48,56},{56,64},{64,7... | collective-permute-start | bytes 786440 | tf_op jit(solution)/shard_map/ppermute | solution.py:42
  307.4 38.3 %collective-permute-start.3 = (bf16[2,128,4,128]{1,3,2,0:T(8,128)(2,1)}, bf16[2,128,4,128]{1,3,2,0:T(8,128)(2,1)}, u32[]{:S(2)}, u32[]{:S(2)}) collective-permute-start(bf16[2,128,4,128]{1,3,2,0:T(8,128)(2,1)} %fusion.18), channel_id=1, source_target_pairs={{8,0},{16,8},{24,16},{32,24},{40,32},{48,40},{56,48},{64,56},{72,6... | collective-permute-start | bytes 786440 | tf_op jit(solution)/shard_map/ppermute | solution.py:42
  337.0 2.9 copy-start.2
  337.0 143.6 %all-reduce.24.cloned.1.call-start = ((), (), s32[]{:S(2)}) async-start(), calls=%async_computation.4 | async-start | bytes 1048576 | tf_op jit(solution)/shard_map/psum | solution.py:32
  339.9 2.5 copy-start.4
  341.2 1.4 copy-start.17
  341.2 2.4 copy-start.13
  397.2 1.3 copy-start.14
  397.2 41.0 %copy-start.5 = (bf16[256,4,128]{0,2,1:T(8,128)(2,1)S(1)}, bf16[256,4,128]{0,2,1:T(8,128)(2,1)}, u32[]{:S(2)}) copy-start(bf16[256,4,128]{0,2,1:T(8,128)(2,1)} %reshape.250) | copy-start | bytes 786436
  397.2 41.0 %copy-start.6 = (bf16[256,4,128]{0,2,1:T(8,128)(2,1)S(1)}, bf16[256,4,128]{0,2,1:T(8,128)(2,1)}, u32[]{:S(2)}) copy-start(bf16[256,4,128]{0,2,1:T(8,128)(2,1)} %reshape.248) | copy-start | bytes 786436
  (5 other events, 4.9 us)
Sparse Core Ops, SparseCore 0:
  67.8 34.5 all-reduce.17
  104.8 54.2 all-reduce.19
  161.5 81.1 all-reduce.21
  303.1 33.8 all-reduce.27
  339.5 57.6 all-reduce.25
  399.5 81.0 all-reduce.23
where the time goes:
time: 491 us; the launch traced here: 490 us
  waiting for transfers between devices  291 us (59%)
  blocking collectives  78.5 us (16%)
  local copies, waits for them, and re-layouts  64.2 us (13%)
  starting transfers between devices  18.6 us (4%)
  between operations  14.8 us (3%)
  matrix products  12.6 us (3%)
  other arithmetic  10.3 us (2%)
    psum x6, waiting for transfers between devices, hpsum(): value = lax.psum(value, name)  263 us
    psum x1, blocking collectives, hpsum(): value = lax.psum(value, name)  39.7 us
    all_gather x3, blocking collectives, hgather(): value = lax.all_gather(value, name, axis=0, tiled=True)  38.8 us
    all_to_all x1, waiting for transfers between devices, local(): lax.all_to_all(stacked, 'head', split_axis=2, concat_axis=1, tiled=True)  28.7 us
    unnamed x45, local copies, waits for them, and re-layouts  20.4 us
    scatter-add x1, local copies, waits for them, and re-layouts, local(): inner = inner.at[:, -1].add(from_right)  12 us
    ppermute x4, starting transfers between devices, shifted(): lax.ppermute(value, seq, [(s, s + steps) for s in range(leading, last)])  11.1 us
    all_to_all x2, local copies, waits for them, and re-layouts, local(): lax.all_to_all(stacked, 'head', split_axis=2, concat_axis=1, tiled=True)  10.2 us
  transfers between devices with their start and end apart: 11, of which 7 were waited for; matrix products, arithmetic and copies ran while one was open for 8% of the time, Pallas kernels for 0%

commit v1 on v0

--- a/solution.py
+++ b/solution.py
@@ -7,6 +7,14 @@
 
 HEAD_DIM = 128
 BLOCK = 128
+
+
+def rest_the_local_data(tile_in, array_dim, out_dim):
+    spare = lax.axis_size("head")
+    u1 = jnp.split(tile_in, spare, axis=array_dim)
+    e_now = jnp.stack(u1, axis=0)
+    opened = lax.all_to_all(e_now, axis_name="head", split_axis=0, concat_axis=0)
+    return jnp.concatenate(opened, axis=out_dim)
 
 
 def seq_parts(mesh):
@@ -43,7 +51,7 @@
 
     def local(query_states, key_states, value_states, out_grad):
         stacked = jnp.stack([query_states, key_states, value_states, out_grad])
-        stacked = lax.all_to_all(stacked, "head", split_axis=2, concat_axis=1, tiled=True)
+        stacked = rest_the_local_data(stacked, 2, 1)
         local_rows = stacked.shape[1]
         head_count = stacked.shape[2] // HEAD_DIM
         block_count = local_rows // BLOCK

time: 491 us -> 474 us (0.965)
  local copies, waits for them, and re-layouts: 64.2 us -> 42.7 us
  waiting for transfers between devices: 291 us -> 298 us
    all_to_all x2 -> x1, local copies, waits for them, and re-layouts: 10.2 us -> 0.1 us  [rest_the_local_data(): lax.all_to_all(e_now, axis_name='head', split_axis=0, concat_axis=0)]
    unnamed x45 -> x44, local copies, waits for them, and re-layouts: 20.4 us -> 12.7 us
    psum x6, waiting for transfers between devices: 263 us -> 269 us  [hpsum(): value = lax.psum(value, name)]
  transfers between devices with their start and end apart: 11 -> 11, of which waited for: 7 -> 7; matrix products, arithmetic and copies ran while one was open for 8% -> 7% of each run, Pallas kernels for 0% -> 0%
where the time goes in v1:
time: 474 us; the launch traced here: 473 us
  waiting for transfers between devices  298 us (63%)
  blocking collectives  78.3 us (17%)
  local copies, waits for them, and re-layouts  42.7 us (9%)
  starting transfers between devices  18.6 us (4%)
  between operations  14.7 us (3%)
  matrix products  11.1 us (2%)
  other arithmetic  10.2 us (2%)
    psum x6, waiting for transfers between devices, hpsum(): value = lax.psum(value, name)  269 us
    psum x1, blocking collectives, hpsum(): value = lax.psum(value, name)  39.4 us
    all_gather x3, blocking collectives, hgather(): value = lax.all_gather(value, name, axis=0, tiled=True)  38.8 us
    all_to_all x1, waiting for transfers between devices, rest_the_local_data(): lax.all_to_all(e_now, axis_name='head', split_axis=0, concat_axis=0)  28.7 us
    unnamed x44, local copies, waits for them, and re-layouts  12.7 us
    scatter-add x1, local copies, waits for them, and re-layouts, local(): inner = inner.at[:, -1].add(from_right)  12 us
    ppermute x4, starting transfers between devices, shifted(): lax.ppermute(value, seq, [(s, s + steps) for s in range(leading, last)])  11.1 us
  transfers between devices with their start and end apart: 11, of which 7 were waited for; matrix products, arithmetic and copies ran while one was open for 7% of the time, Pallas kernels for 0%

profile of v1, /device:TPU:2, one launch (start us, length us, event | category | flops | bytes accessed | tf_op | source)
XLA Modules:
  0.0 473.3 jit_solution(3017845734140277190)
XLA Ops:
  13.8 7.1 %all-to-all-start = ((bf16[8,4,32,512]{3,2,1,0:T(8,128)(2,1)}), bf16[8,4,32,512]{3,2,1,0:T(8,128)(2,1)S(1)}, u32[]{:S(2)}, u32[]{:S(2)}) async-start(bf16[8,4,32,512]{3,2,1,0:T(8,128)(2,1)} %fusion.31), calls=%async_computation | async-start | bytes 2097152 | tf_op jit(solution)/shard_map/all_to_all | solution.py:16
  20.9 28.7 %all-to-all-done = bf16[8,4,32,512]{3,2,1,0:T(8,128)(2,1)S(1)} async-done(((bf16[8,4,32,512]{3,2,1,0:T(8,128)(2,1)}), bf16[8,4,32,512]{3,2,1,0:T(8,128)(2,1)S(1)}, u32[]{:S(2)}, u32[]{:S(2)}) %all-to-all-start) | async-done | bytes 1048608 | tf_op jit(solution)/shard_map/all_to_all | solution.py:16
  50.7 34.6 %all-reduce.18.cloned.1.call-done = bf16[4,128,512]{2,1,0:T(8,128)(2,1)} async-done(((bf16[4,128,512]{2,1,0:T(8,128)(2,1)}), bf16[4,128,512]{2,1,0:T(8,128)(2,1)}) %all-reduce.18.cloned.1.call-update) | async-done | bytes 524304 | tf_op jit(solution)/shard_map/psum | solution.py:40
  86.3 2.2 collective-permute-start
  88.5 3.4 collective-permute-start.1
  91.8 50.1 %all-reduce.20.cloned.1.call-done = bf16[4,128,512]{2,1,0:T(8,128)(2,1)} async-done(((bf16[4,128,512]{2,1,0:T(8,128)(2,1)}), bf16[4,128,512]{2,1,0:T(8,128)(2,1)}) %all-reduce.20.cloned.1.call-update) | async-done | bytes 524304 | tf_op jit(solution)/shard_map/psum | solution.py:40
  146.9 78.7 %all-reduce.22.cloned.1.call-done = bf16[4,128,512]{2,1,0:T(8,128)(2,1)} async-done(((bf16[4,128,512]{2,1,0:T(8,128)(2,1)}), bf16[4,128,512]{2,1,0:T(8,128)(2,1)}) %all-reduce.22.cloned.1.call-update) | async-done | bytes 524304 | tf_op jit(solution)/shard_map/psum | solution.py:40
  228.8 1.8 all-gather
  230.6 11.9 %all_gather.10 = f32[8,3,4,128]{3,2,1,0:T(4,128)S(1)} all-gather(f32[2,3,4,128]{3,2,1,0:T(4,128)S(1)} %bitcast.202), channel_id=1, replica_groups=mesh['sz'=8,'sx'=4,'sc'=2,'head'=8] {'sx'}, dimensions={0}, use_global_device_ids=true | all-gather | bytes 61440 | tf_op jit(solution)/shard_map/all_gather | solution.py:45
  242.5 25.1 %all_gather.11 = f32[64,3,4,128]{3,2,1,0:T(4,128)S(1)} all-gather(f32[8,3,4,128]{3,2,1,0:T(4,128)S(1)} %all_gather.10), channel_id=1, replica_groups=mesh['sz'=8,'sx'=4,'sc'=2,'head'=8] {'sz'}, dimensions={0}, use_global_device_ids=true | all-gather | bytes 442368 | tf_op jit(solution)/shard_map/all_gather | solution.py:45
  274.0 1.6 multiply_convert_fusion
  275.5 1.7 stack.99
  277.3 1.6 multiply_bitcast_fusion
  278.9 1.7 stack.98
  280.7 2.0 copy_dynamic-update-slice_fusion.1
  283.4 1.7 copy-done
  287.7 1.9 collective-permute-start.2
  290.4 3.6 collective-permute-start.3
  294.0 25.9 %all-reduce.28.cloned.1.call-done = (f32[128,4,128]{0,2,1:T(8,128)}, f32[128,4,128]{0,2,1:T(8,128)}, f32[128,4,128]{0,2,1:T(8,128)}, f32[128,4,128]{0,2,1:T(8,128)}) async-done(((f32[128,4,128]{0,2,1:T(8,128)}, f32[128,4,128]{0,2,1:T(8,128)}, f32[128,4,128]{0,2,1:T(8,128)}, f32[128,4,128]{0,2,1:T(8,128)}), (f32[128,4,128]{0,2,1:T(8,128)}, f32[128,4,128]{0,2,1:T(8,128)}, f32[128,4,128]{0,2,1:T(8,128)}, ...) | async-done | bytes 1048592 | tf_op jit(solution)/shard_map/psum | solution.py:40
  320.2 1.9 fusion.1
  328.7 12.0 %scatter-add.9 = f32[2,2,128,4,128]{2,1,4,3,0:T(2,128)S(1)} dynamic-update-slice(f32[2,2,128,4,128]{2,1,4,3,0:T(2,128)S(1)} %copy.100, f32[2,1,128,4,128]{2,1,4,3,0:T(1,128)S(1)} %add.147, s32[]{:T(128)} %constant.93.clone.1, s32[]{:T(128)} %constant.98.clone.1, s32[]{:T(128)} %constant.93.clone.1, s32[]{:T(128)} %constant.93.clone.1, s32[]{:T(128)} %constant.93.clone.1) | dynamic-update-slice | bytes 1048580 | tf_op jit(solution)/shard_map/scatter-add | solution.py:207
  341.6 38.6 %all-reduce.26.cloned.1.call-done = (f32[128,4,128]{0,2,1:T(8,128)}, f32[128,4,128]{0,2,1:T(8,128)}, f32[128,4,128]{0,2,1:T(8,128)}, f32[128,4,128]{0,2,1:T(8,128)}) async-done(((f32[128,4,128]{0,2,1:T(8,128)}, f32[128,4,128]{0,2,1:T(8,128)}, f32[128,4,128]{0,2,1:T(8,128)}, f32[128,4,128]{0,2,1:T(8,128)}), (f32[128,4,128]{0,2,1:T(8,128)}, f32[128,4,128]{0,2,1:T(8,128)}, f32[128,4,128]{0,2,1:T(8,128)}, ...) | async-done | bytes 1048592 | tf_op jit(solution)/shard_map/psum | solution.py:40
  380.4 39.4 %all-reduce.29 = (bf16[128,4,128]{0,2,1:T(8,128)(2,1)S(1)}, bf16[128,4,128]{0,2,1:T(8,128)(2,1)S(1)}) all-reduce(f32[128,4,128]{0,2,1:T(8,128)} %get-tuple-element.46, f32[128,4,128]{0,2,1:T(8,128)} %get-tuple-element.47), channel_id=1, replica_groups=mesh['sz'=8,'sx'=4,'sc'=2,'head'=8] {'sz'}, use_global_device_ids=true, to_apply=%region_10.11 | all-reduce | flops 131072 | bytes 786432 | tf_op jit(solution)/shard_map/psum | solution.py:40
  422.6 41.0 %all-reduce.24.cloned.1.call-done = (f32[128,4,128]{0,2,1:T(8,128)}, f32[128,4,128]{0,2,1:T(8,128)}) async-done(((f32[128,4,128]{0,2,1:T(8,128)}, f32[128,4,128]{0,2,1:T(8,128)}), (f32[128,4,128]{0,2,1:T(8,128)}, f32[128,4,128]{0,2,1:T(8,128)})) %all-reduce.24.cloned.1.call-update) | async-done | bytes 524304 | tf_op jit(solution)/shard_map/psum | solution.py:40
  (137 shorter events, 40.1 us)
Async XLA Ops:
  13.8 35.8 %all-to-all-start = ((bf16[8,4,32,512]{3,2,1,0:T(8,128)(2,1)}), bf16[8,4,32,512]{3,2,1,0:T(8,128)(2,1)S(1)}, u32[]{:S(2)}, u32[]{:S(2)}) async-start(bf16[8,4,32,512]{3,2,1,0:T(8,128)(2,1)} %fusion.31), calls=%async_computation | async-start | bytes 2097152 | tf_op jit(solution)/shard_map/all_to_all | solution.py:16
  20.9 64.4 %all-reduce.18.cloned.1.call-start = ((), (), s32[]{:S(2)}) async-start(), calls=%async_computation.1 | async-start | bytes 1048576 | tf_op jit(solution)/shard_map/psum | solution.py:40
  50.6 91.4 %all-reduce.20.cloned.1.call-start = ((), (), s32[]{:S(2)}) async-start(), calls=%async_computation.2 | async-start | bytes 1048576 | tf_op jit(solution)/shard_map/psum | solution.py:40
  85.3 140.3 %all-reduce.22.cloned.1.call-start = ((), (), s32[]{:S(2)}) async-start(), calls=%async_computation.3 | async-start | bytes 1048576 | tf_op jit(solution)/shard_map/psum | solution.py:40
  86.3 57.6 %collective-permute-start = (bf16[2,128,512]{2,1,0:T(8,128)(2,1)}, bf16[2,128,512]{2,1,0:T(8,128)(2,1)}, u32[]{:S(2)}, u32[]{:S(2)}) collective-permute-start(bf16[2,128,512]{2,1,0:T(8,128)(2,1)} %get-tuple-element.77), channel_id=1, source_target_pairs={{0,8},{8,16},{16,24},{24,32},{32,40},{40,48},{48,56},{56,64},{64,7... | collective-permute-start | bytes 786440 | tf_op jit(solution)/shard_map/ppermute | solution.py:50
  88.5 55.4 %collective-permute-start.1 = (bf16[2,128,512]{2,1,0:T(8,128)(2,1)S(1)}, bf16[2,128,512]{2,1,0:T(8,128)(2,1)}, u32[]{:S(2)}, u32[]{:S(2)}) collective-permute-start(bf16[2,128,512]{2,1,0:T(8,128)(2,1)S(1)} %get-tuple-element.78), channel_id=1, source_target_pairs={{8,0},{16,8},{24,16},{32,24},{40,32},{48,40},{56,48},{64,56},{72,6... | collective-permute-start | bytes 786440 | tf_op jit(solution)/shard_map/ppermute | solution.py:50
  142.0 178.0 %all-reduce.28.cloned.1.call-start = ((), (), s32[]{:S(2)}) async-start(), calls=%async_computation.6 | async-start | bytes 2097152 | tf_op jit(solution)/shard_map/psum | solution.py:40
  143.6 126.5 %copy-start.8 = (bf16[2,128,4,128]{3,1,2,0:T(8,128)(2,1)}, bf16[2,128,4,128]{3,1,2,0:T(8,128)(2,1)S(1)}, u32[]{:S(2)}) copy-start(bf16[2,128,4,128]{3,1,2,0:T(8,128)(2,1)S(1)} %copy.85) | copy-start | bytes 786436
  145.1 125.0 %copy-start.9 = (bf16[2,128,4,128]{3,1,2,0:T(8,128)(2,1)}, bf16[2,128,4,128]{3,1,2,0:T(8,128)(2,1)S(1)}, u32[]{:S(2)}) copy-start(bf16[2,128,4,128]{3,1,2,0:T(8,128)(2,1)S(1)} %copy.84) | copy-start | bytes 786436
  146.9 123.3 %copy-start.10 = (bf16[2,128,4,128]{3,1,2,0:T(8,128)(2,1)}, bf16[2,128,4,128]{3,1,2,0:T(8,128)(2,1)S(1)}, u32[]{:S(2)}) copy-start(bf16[2,128,4,128]{3,1,2,0:T(8,128)(2,1)S(1)} %copy.86) | copy-start | bytes 786436
  227.8 41.1 %copy-start.3 = (bf16[1,128,512]{1,2,0:T(8,128)(2,1)}, bf16[1,128,512]{1,2,0:T(8,128)(2,1)S(1)}, u32[]{:S(2)}) copy-start(bf16[1,128,512]{1,2,0:T(8,128)(2,1)S(1)} %copy.71) | copy-start | bytes 393220
  271.5 1.0 copy-start.11
  271.5 1.1 copy-start.13
  271.6 1.2 copy-start.14
  280.7 2.2 copy-start.1
  283.2 2.0 copy-start
  286.0 94.3 %all-reduce.26.cloned.1.call-start = ((), (), s32[]{:S(2)}) async-start(), calls=%async_computation.5 | async-start | bytes 2097152 | tf_op jit(solution)/shard_map/psum | solution.py:40
  287.7 38.5 %collective-permute-start.2 = (bf16[2,128,4,128]{1,3,2,0:T(8,128)(2,1)}, bf16[2,128,4,128]{1,3,2,0:T(8,128)(2,1)S(1)}, u32[]{:S(2)}, u32[]{:S(2)}) collective-permute-start(bf16[2,128,4,128]{1,3,2,0:T(8,128)(2,1)} %fusion.17), channel_id=1, source_target_pairs={{0,8},{8,16},{16,24},{24,32},{32,40},{40,48},{48,56},{56,64},{64,7... | collective-permute-start | bytes 786440 | tf_op jit(solution)/shard_map/ppermute | solution.py:50
  290.4 36.8 %collective-permute-start.3 = (bf16[2,128,4,128]{1,3,2,0:T(8,128)(2,1)}, bf16[2,128,4,128]{1,3,2,0:T(8,128)(2,1)}, u32[]{:S(2)}, u32[]{:S(2)}) collective-permute-start(bf16[2,128,4,128]{1,3,2,0:T(8,128)(2,1)} %fusion.18), channel_id=1, source_target_pairs={{8,0},{16,8},{24,16},{32,24},{40,32},{48,40},{56,48},{64,56},{72,6... | collective-permute-start | bytes 786440 | tf_op jit(solution)/shard_map/ppermute | solution.py:50
  320.0 2.2 copy-start.2
  320.0 143.7 %all-reduce.24.cloned.1.call-start = ((), (), s32[]{:S(2)}) async-start(), calls=%async_computation.4 | async-start | bytes 1048576 | tf_op jit(solution)/shard_map/psum | solution.py:40
  322.1 1.7 copy-start.4
  323.5 1.6 copy-start.12
  380.2 39.6 %copy-start.5 = (bf16[256,4,128]{0,2,1:T(8,128)(2,1)S(1)}, bf16[256,4,128]{0,2,1:T(8,128)(2,1)}, u32[]{:S(2)}) copy-start(bf16[256,4,128]{0,2,1:T(8,128)(2,1)} %reshape.258) | copy-start | bytes 786436
  (2 other events, 1.6 us)
Sparse Core Ops, SparseCore 0:
  50.7 34.5 all-reduce.17
  87.7 54.2 all-reduce.19
  144.4 81.1 all-reduce.21
  286.1 33.8 all-reduce.27
  322.5 57.7 all-reduce.25
  382.5 81.1 all-reduce.23
